TPU v7x, 768 devices: a whole 4x8x12 slice. The times are simulated.
768 devices in a mesh: lat: 24 (over z_lo, x, core), lon: 32 (over y, z_hi).
Axes of the slice: x: 4, y: 8, z: 12 (z_hi: 4, z_lo: 3; z = z_hi * 3 + z_lo), core: 2. Of those that a mesh axis runs over, the one named last changes fastest.
Arguments:
- fields: bfloat16 [384, 512, 1024], P('lat', 'lon'), may hold values from -6 to 6
- gain_conv: float32 [1024], replicated, may hold values from 0.1 to 1.9
- w_depth: float32 [7, 7, 1024], replicated, may hold values from -0.875 to 0.875
- w_layer: bfloat16 [1024, 3072], P(None, 'lat'), as said below
- gain_attn: float32 [1024], replicated, may hold values from 0.1 to 1.9
- gain_out: float32 [1024], replicated, may hold values from 0.1 to 1.9
Outputs:
- layer_out: bfloat16 [384, 512, 1024], P('lat', 'lon')
Inputs may be any that keep to these rules, and one draw needn't show every extreme that they name: `w_layer`: independent entries of mean zero; the scale of a column lies between 1 / sqrt(1024) and 20 / sqrt(1024), and no entry exceeds 80 / sqrt(1024) in magnitude.
All inputs are finite; a program needn't handle non-finite values.
Results may differ from a plain program's by a relative error of at most 0.012.
The roundings to bfloat16 on the way count: a program that leaves them out, or rounds other values in their place, can miss the bound.
Values may be sent and summed in bfloat16 or wider, within the bound.
A program may use at most 32 MiB of HBM per device.

v0:
```python
import jax
import jax.numpy as jnp
from jax import lax
from jax.sharding import PartitionSpec as P

HEAD_DIM = 64
KERNEL = 7
REACH = 3


epsilon = 1e-06


def padded_2(value, sides, width, wrap):
    for axis, dim in sides:
        peers, length = (lax.axis_size(axis), value.shape[dim])
        up = [(i, (i + 1) % peers) for i in range(peers if wrap else peers - 1)]
        down = [(j, i) for i, j in up]
        last = lax.slice_in_dim(value, length - width, length, axis=dim)
        leading = lax.slice_in_dim(value, 0, width, axis=dim)
        before = lax.ppermute(last, axis, up)
        after = lax.ppermute(leading, axis, down)
        value = jnp.concatenate([before, value, after], axis=dim)
    return value


def passed_along(block, axis, distance):
    devices = range(lax.axis_size(axis))
    route = [((i - distance) % len(devices), i) for i in devices]
    return lax.ppermute(block, axis, route)


def rms_scale(values, gain):
    return values * lax.rsqrt(jnp.mean(values * values, axis=-1, keepdims=True) + epsilon) * gain


def depthwise(padded, w_depth, lat_rows, lon_cols):
    total = jnp.zeros((lat_rows, lon_cols, padded.shape[2]), jnp.float32)
    for row_off in range(KERNEL):
        for col_off in range(KERNEL):
            window = padded[row_off : row_off + lat_rows, col_off : col_off + lon_cols].astype(
                jnp.float32
            )
            total = total + window * w_depth[row_off, col_off]
    return total


def attend(queries, everything, channels):
    tokens = queries.shape[0]
    groups = channels // (2 * HEAD_DIM)
    qgroup = queries.reshape(tokens, groups, 2, HEAD_DIM).transpose(1, 0, 2, 3)
    keys = everything[:, : channels // 2].reshape(-1, groups, HEAD_DIM).transpose(1, 0, 2)
    values = everything[:, channels // 2 :].reshape(-1, groups, HEAD_DIM).transpose(1, 0, 2)

    def one_group(operands):
        qpart, kpart, vpart = operands
        scores = jnp.einsum(
            "tpd,kd->ptk", qpart, kpart, preferred_element_type=jnp.float32
        ) * HEAD_DIM ** (-0.5)
        peak = jnp.max(scores, axis=-1, keepdims=True)
        expo = jnp.exp(scores - peak)
        probs = (expo / jnp.sum(expo, axis=-1, keepdims=True)).astype(jnp.bfloat16)
        return jnp.einsum("ptk,kd->tpd", probs, vpart, preferred_element_type=jnp.float32)

    result = lax.map(one_group, (qgroup, keys, values))
    return result.transpose(1, 0, 2, 3).reshape(tokens, channels)


def per_device(fields, gain_conv, w_depth, w_layer, gain_attn, gain_out):
    lat_rows, lon_cols, channels = fields.shape
    weights_all = lax.all_gather(w_layer, "lat", axis=1, tiled=True)
    field_float = fields.astype(jnp.float32)
    normed = rms_scale(field_float, gain_conv).astype(jnp.bfloat16)
    banded = padded_2(normed, (("lat", 0),), REACH, False)
    padded = padded_2(banded, (("lon", 1),), REACH, True)
    conv_out = depthwise(padded, w_depth, lat_rows, lon_cols).astype(jnp.bfloat16)
    conv_flat = conv_out.reshape(lat_rows * lon_cols, channels)
    mixed = field_float.reshape(-1, channels) + jnp.dot(
        conv_flat, weights_all[:, :channels], preferred_element_type=jnp.float32
    )
    attn_in = rms_scale(mixed, gain_attn).astype(jnp.bfloat16)
    projected = jnp.dot(
        attn_in, weights_all[:, channels:], preferred_element_type=jnp.float32
    ).astype(jnp.bfloat16)
    queries = projected[:, :channels]
    kv_sheet = projected[:, channels:].reshape(lat_rows, lon_cols, channels)
    pieces = [projected[:, channels:]]
    for offset in (1, 2, -1, -2):
        arrived = passed_along(kv_sheet, "lon", offset)
        pieces.append(arrived.reshape(-1, channels))
    everything = jnp.concatenate(pieces, axis=0)
    attended = attend(queries, everything, channels)
    result = mixed + rms_scale(attended, gain_out)
    return result.astype(jnp.bfloat16).reshape(lat_rows, lon_cols, channels)


def solution(mesh):
    return jax.shard_map(
        per_device,
        mesh=mesh,
        in_specs=(P("lat", "lon", None), P(), P(), P(None, "lat"), P(), P()),
        out_specs=P("lat", "lon", None),
        check_vma=False,
    )
```

profile of v0, /device:TPU:76, one launch (start us, length us, event | category | flops | bytes accessed | tf_op | source)
XLA Modules:
  0.0 302.1 jit_solution(4108704124735867296)
XLA Ops:
  11.7 3.6 %collective-permute-start.1 = (bf16[3,16,1024]{2,1,0:T(8,128)(2,1)S(1)}, bf16[3,16,1024]{2,1,0:T(8,128)(2,1)S(1)}, u32[]{:S(2)}, u32[]{:S(2)}) collective-permute-start(bf16[3,16,1024]{2,1,0:T(8,128)(2,1)S(1)} %get-tuple-element.53), channel_id=1, source_target_pairs={{32,0},{64,32},{96,64},{128,96},{160,128},{192,160},{224,192},{256... | collective-permute-start | bytes 294920 | tf_op jit(solution)/shard_map/ppermute | solution.py:22
  17.7 9.1 %collective-permute-start.2 = (bf16[22,3,1024]{2,1,0:T(4,128)(2,1)S(1)}, bf16[22,3,1024]{2,1,0:T(4,128)(2,1)S(1)}, u32[]{:S(2)}, u32[]{:S(2)}) collective-permute-start(bf16[22,3,1024]{2,1,0:T(4,128)(2,1)S(1)} %get-tuple-element.50), channel_id=1, source_target_pairs={{0,1},{1,2},{2,3},{3,4},{4,5},{5,6},{6,7},{7,8},{8,9},{9,10},{10,1... | collective-permute-start | bytes 405512 | tf_op jit(solution)/shard_map/ppermute | solution.py:21
  26.8 6.4 %collective-permute-start.3 = (bf16[22,3,1024]{2,1,0:T(4,128)(2,1)S(1)}, bf16[22,3,1024]{2,1,0:T(4,128)(2,1)S(1)}, u32[]{:S(2)}, u32[]{:S(2)}) collective-permute-start(bf16[22,3,1024]{2,1,0:T(4,128)(2,1)S(1)} %get-tuple-element.51), channel_id=1, source_target_pairs={{1,0},{2,1},{3,2},{4,3},{5,4},{6,5},{7,6},{8,7},{9,8},{10,9},{11,1... | collective-permute-start | bytes 405512 | tf_op jit(solution)/shard_map/ppermute | solution.py:22
  33.2 8.2 %collective-permute-done.2 = bf16[22,3,1024]{2,1,0:T(4,128)(2,1)S(1)} collective-permute-done((bf16[22,3,1024]{2,1,0:T(4,128)(2,1)S(1)}, bf16[22,3,1024]{2,1,0:T(4,128)(2,1)S(1)}, u32[]{:S(2)}, u32[]{:S(2)}) %collective-permute-start.2) | collective-permute-done | bytes 135200 | tf_op jit(solution)/shard_map/ppermute | solution.py:21
  41.4 2.6 collective-permute-done.3
  44.7 8.6 %add_convert_fusion.1 = bf16[16,16,1024]{2,1,0:T(8,128)(2,1)S(1)} fusion(bf16[16,16,1024]{2,1,0:T(8,128)(2,1)S(1)} %multiply_convert_fusion.1, bf16[3,16,1024]{2,1,0:T(8,128)(2,1)S(1)} %collective-permute-done.1, bf16[3,16,1024]{2,1,0:T(8,128)(2,1)S(1)} %collective-permute-done, bf16[22,19,1024]{2,1,0:T(8,128)(2,1)S(1)} %get-tuple-element.49, ...), kind=kLoop, calls=%fused_computation.41 | loop fusion | flops 40108032 | bytes 23465984 | tf_op jit(solution)/shard_map/convert_element_type | solution.py:76
  53.3 62.8 %all-gather.2.cloned.1.call-done = bf16[1024,3072]{1,0:T(8,128)(2,1)} async-done(((bf16[1024,128]{1,0:T(8,128)(2,1)}), bf16[1024,3072]{1,0:T(8,128)(2,1)}) %all-gather.2.cloned.1.call-update) | async-done | bytes 6291472 | tf_op jit(solution)/shard_map/all_gather | solution.py:71
  116.1 2.4 multiply_reduce_fusion
  118.5 3.9 %fusion.46 = bf16[256,2048]{1,0:T(8,128)(2,1)S(1)} fusion(bf16[1024,3072]{1,0:T(8,128)(2,1)} %all-gather.2.cloned.1.call-done, f32[256,1024]{1,0:T(8,128)S(1)} %get-tuple-element.104, f32[1024]{0:T(1024)S(1)} %copy-done.6, f32[256]{0:T(256)S(1)} %add_rsqrt_fusion.2), kind=kOutput, calls=%fused_computation.30 | convolution fusion | flops 1075052544 | bytes 6296576 | tf_op jit(solution)/shard_map/dot_general | solution.py:82
  123.4 11.1 %collective-permute-start.4 = (bf16[16,16,1024]{2,1,0:T(8,128)(2,1)S(1)}, bf16[16,16,1024]{2,1,0:T(8,128)(2,1)}, u32[]{:S(2)}, u32[]{:S(2)}) collective-permute-start(bf16[16,16,1024]{2,1,0:T(8,128)(2,1)S(1)} %bitcast.144), channel_id=1, source_target_pairs={{31,0},{0,1},{1,2},{2,3},{3,4},{4,5},{5,6},{6,7},{7,8},{8,9},{9,10... | collective-permute-start | bytes 1572872 | tf_op jit(solution)/shard_map/ppermute | solution.py:30
  134.5 5.9 %collective-permute-start.5 = (bf16[16,16,1024]{2,1,0:T(8,128)(2,1)S(1)}, bf16[16,16,1024]{2,1,0:T(8,128)(2,1)S(1)}, u32[]{:S(2)}, u32[]{:S(2)}) collective-permute-start(bf16[16,16,1024]{2,1,0:T(8,128)(2,1)S(1)} %bitcast.145), channel_id=1, source_target_pairs={{30,0},{31,1},{0,2},{1,3},{2,4},{3,5},{4,6},{5,7},{6,8},{7,9},{8,1... | collective-permute-start | bytes 1572872 | tf_op jit(solution)/shard_map/ppermute | solution.py:30
  140.4 7.2 %collective-permute-start.6 = (bf16[16,16,1024]{2,1,0:T(8,128)(2,1)S(1)}, bf16[16,16,1024]{2,1,0:T(8,128)(2,1)S(1)}, u32[]{:S(2)}, u32[]{:S(2)}) collective-permute-start(bf16[16,16,1024]{2,1,0:T(8,128)(2,1)S(1)} %bitcast.146), channel_id=1, source_target_pairs={{1,0},{2,1},{3,2},{4,3},{5,4},{6,5},{7,6},{8,7},{9,8},{10,9},{11,1... | collective-permute-start | bytes 1572872 | tf_op jit(solution)/shard_map/ppermute | solution.py:30
  149.8 14.9 %collective-permute-done.4 = bf16[16,16,1024]{2,1,0:T(8,128)(2,1)} collective-permute-done((bf16[16,16,1024]{2,1,0:T(8,128)(2,1)S(1)}, bf16[16,16,1024]{2,1,0:T(8,128)(2,1)}, u32[]{:S(2)}, u32[]{:S(2)}) %collective-permute-start.4) | collective-permute-done | bytes 524320 | tf_op jit(solution)/shard_map/ppermute | solution.py:30
  168.0 29.3 %collective-permute-done.6 = bf16[16,16,1024]{2,1,0:T(8,128)(2,1)S(1)} collective-permute-done((bf16[16,16,1024]{2,1,0:T(8,128)(2,1)S(1)}, bf16[16,16,1024]{2,1,0:T(8,128)(2,1)S(1)}, u32[]{:S(2)}, u32[]{:S(2)}) %collective-permute-start.6) | collective-permute-done | bytes 524320 | tf_op jit(solution)/shard_map/ppermute | solution.py:30
  198.2 54.0 %collective-permute-done.7 = bf16[16,16,1024]{2,1,0:T(8,128)(2,1)S(1)} collective-permute-done((bf16[16,16,1024]{2,1,0:T(8,128)(2,1)S(1)}, bf16[16,16,1024]{2,1,0:T(8,128)(2,1)S(1)}, u32[]{:S(2)}, u32[]{:S(2)}) %collective-permute-start.7) | collective-permute-done | bytes 524320 | tf_op jit(solution)/shard_map/ppermute | solution.py:30
  257.8 35.2 %while.10 = (s32[]{:T(128)}, f32[8,256,2,64]{1,3,2,0:T(8,128)S(1)}, bf16[8,1280,64]{1,2,0:T(8,128)(2,1)}, bf16[8,1280,64]{1,2,0:T(8,128)(2,1)}, bf16[8,256,2,64]{1,3,2,0:T(8,128)(2,1)S(1)}, /*index=5*/s32[]{:T(128)}) while((s32[]{:T(128)}, f32[8,256,2,64]{1,3,2,0:T(8,128)S(1)}, bf16[8,1280,64]{1,2,0:T(8,128)(2,1)}, ...), condition=%wide.region_5.6_spmd, body=%wide.region_2.5_spmd.sunk | while | flops 256248832 | bytes 760901 | solution.py:65
  259.8 2.4 fusion.86
  264.2 2.4 fusion.86
  268.6 2.4 fusion.86
  273.0 2.4 fusion.86
  277.4 2.4 fusion.86
  281.8 2.4 fusion.86
  286.2 2.4 fusion.86
  290.6 2.4 fusion.86
  (53 shorter events, 38.8 us)
Async XLA Ops:
  6.5 8.8 %copy-start.4 = (f32[7,7,1024]{2,1,0:T(8,128)S(1)}, f32[7,7,1024]{2,1,0:T(8,128)}, u32[]{:S(2)}) copy-start(f32[7,7,1024]{2,1,0:T(8,128)} %param.10) | copy-start | bytes 602116
  6.5 109.6 %all-gather.2.cloned.1.call-start = ((), (), s32[]{:S(2)}) async-start(), calls=%async_computation | async-start | bytes 6553600 | tf_op jit(solution)/shard_map/all_gather | solution.py:71
  9.8 5.9 %collective-permute-start = (bf16[3,16,1024]{2,1,0:T(8,128)(2,1)S(1)}, bf16[3,16,1024]{2,1,0:T(8,128)(2,1)S(1)}, u32[]{:S(2)}, u32[]{:S(2)}) collective-permute-start(bf16[3,16,1024]{2,1,0:T(8,128)(2,1)S(1)} %get-tuple-element.52), channel_id=1, source_target_pairs={{0,32},{32,64},{64,96},{96,128},{128,160},{160,192},{192,224},{224... | collective-permute-start | bytes 294920 | tf_op jit(solution)/shard_map/ppermute | solution.py:21
  11.7 5.8 %collective-permute-start.1 = (bf16[3,16,1024]{2,1,0:T(8,128)(2,1)S(1)}, bf16[3,16,1024]{2,1,0:T(8,128)(2,1)S(1)}, u32[]{:S(2)}, u32[]{:S(2)}) collective-permute-start(bf16[3,16,1024]{2,1,0:T(8,128)(2,1)S(1)} %get-tuple-element.53), channel_id=1, source_target_pairs={{32,0},{64,32},{96,64},{128,96},{160,128},{192,160},{224,192},{256... | collective-permute-start | bytes 294920 | tf_op jit(solution)/shard_map/ppermute | solution.py:22
  17.7 23.7 %collective-permute-start.2 = (bf16[22,3,1024]{2,1,0:T(4,128)(2,1)S(1)}, bf16[22,3,1024]{2,1,0:T(4,128)(2,1)S(1)}, u32[]{:S(2)}, u32[]{:S(2)}) collective-permute-start(bf16[22,3,1024]{2,1,0:T(4,128)(2,1)S(1)} %get-tuple-element.50), channel_id=1, source_target_pairs={{0,1},{1,2},{2,3},{3,4},{4,5},{5,6},{6,7},{7,8},{8,9},{9,10},{10,1... | collective-permute-start | bytes 405512 | tf_op jit(solution)/shard_map/ppermute | solution.py:21
  26.8 17.2 %collective-permute-start.3 = (bf16[22,3,1024]{2,1,0:T(4,128)(2,1)S(1)}, bf16[22,3,1024]{2,1,0:T(4,128)(2,1)S(1)}, u32[]{:S(2)}, u32[]{:S(2)}) collective-permute-start(bf16[22,3,1024]{2,1,0:T(4,128)(2,1)S(1)} %get-tuple-element.51), channel_id=1, source_target_pairs={{1,0},{2,1},{3,2},{4,3},{5,4},{6,5},{7,6},{8,7},{9,8},{10,9},{11,1... | collective-permute-start | bytes 405512 | tf_op jit(solution)/shard_map/ppermute | solution.py:22
  44.7 71.4 %copy-start.1 = (bf16[16,16,1024]{2,1,0:T(8,128)(2,1)S(1)}, bf16[16,16,1024]{2,1,0:T(8,128)(2,1)}, u32[]{:S(2)}) copy-start(bf16[16,16,1024]{2,1,0:T(8,128)(2,1)} %param.8) | copy-start | bytes 1572868
  116.1 2.4 copy-start.6
  118.5 3.9 %copy-start.2 = (f32[256,1024]{1,0:T(8,128)}, f32[256,1024]{1,0:T(8,128)S(1)}, u32[]{:S(2)}) copy-start(f32[256,1024]{1,0:T(8,128)S(1)} %get-tuple-element.104) | copy-start | bytes 3145732
  123.4 41.3 %collective-permute-start.4 = (bf16[16,16,1024]{2,1,0:T(8,128)(2,1)S(1)}, bf16[16,16,1024]{2,1,0:T(8,128)(2,1)}, u32[]{:S(2)}, u32[]{:S(2)}) collective-permute-start(bf16[16,16,1024]{2,1,0:T(8,128)(2,1)S(1)} %bitcast.144), channel_id=1, source_target_pairs={{31,0},{0,1},{1,2},{2,3},{3,4},{4,5},{5,6},{6,7},{7,8},{8,9},{9,10... | collective-permute-start | bytes 1572872 | tf_op jit(solution)/shard_map/ppermute | solution.py:30
  134.5 32.6 %collective-permute-start.5 = (bf16[16,16,1024]{2,1,0:T(8,128)(2,1)S(1)}, bf16[16,16,1024]{2,1,0:T(8,128)(2,1)S(1)}, u32[]{:S(2)}, u32[]{:S(2)}) collective-permute-start(bf16[16,16,1024]{2,1,0:T(8,128)(2,1)S(1)} %bitcast.145), channel_id=1, source_target_pairs={{30,0},{31,1},{0,2},{1,3},{2,4},{3,5},{4,6},{5,7},{6,8},{7,9},{8,1... | collective-permute-start | bytes 1572872 | tf_op jit(solution)/shard_map/ppermute | solution.py:30
  140.4 56.9 %collective-permute-start.6 = (bf16[16,16,1024]{2,1,0:T(8,128)(2,1)S(1)}, bf16[16,16,1024]{2,1,0:T(8,128)(2,1)S(1)}, u32[]{:S(2)}, u32[]{:S(2)}) collective-permute-start(bf16[16,16,1024]{2,1,0:T(8,128)(2,1)S(1)} %bitcast.146), channel_id=1, source_target_pairs={{1,0},{2,1},{3,2},{4,3},{5,4},{6,5},{7,6},{8,7},{9,8},{10,9},{11,1... | collective-permute-start | bytes 1572872 | tf_op jit(solution)/shard_map/ppermute | solution.py:30
  147.7 104.5 %collective-permute-start.7 = (bf16[16,16,1024]{2,1,0:T(8,128)(2,1)S(1)}, bf16[16,16,1024]{2,1,0:T(8,128)(2,1)S(1)}, u32[]{:S(2)}, u32[]{:S(2)}) collective-permute-start(bf16[16,16,1024]{2,1,0:T(8,128)(2,1)S(1)} %bitcast.147), channel_id=1, source_target_pairs={{2,0},{3,1},{4,2},{5,3},{6,4},{7,5},{8,6},{9,7},{10,8},{11,9},{12,... | collective-permute-start | bytes 1572872 | tf_op jit(solution)/shard_map/ppermute | solution.py:30
  256.4 1.4 copy-start
  293.0 1.2 copy-start.3
  293.0 1.2 copy-start.5
Sparse Core Ops, SparseCore 0:
  9.7 106.3 all-gather.1
where the time goes:
time: 303 us; the launch traced here: 302 us
  waiting for transfers between devices  175 us (58%)
  starting transfers between devices  47.2 us (16%)
  matrix products  41.4 us (14%)
  between operations  13.6 us (4%)
  other arithmetic  13 us (4%)
  local copies, waits for them, and re-layouts  11.6 us (4%)
    ppermute x4, waiting for transfers between devices, passed_along(): return lax.ppermute(block, axis, route)  98.8 us
    all_gather x1, waiting for transfers between devices, per_device(): weights_all = lax.all_gather(w_layer, 'lat', axis=1, tiled=True)  62.8 us
    ppermute x4, starting transfers between devices, passed_along(): return lax.ppermute(block, axis, route)  26.2 us
    dot_general x8, matrix products, one_group(): jnp.einsum('ptk,kd->tpd', probs, vpart, preferred_element_type=jnp.float32)  19.4 us
    sub x8, matrix products, one_group(): expo = jnp.exp(scores - peak)  15.7 us
    ppermute x2, starting transfers between devices, padded_2(): before = lax.ppermute(last, axis, up)  11 us
    ppermute x2, starting transfers between devices, padded_2(): after = lax.ppermute(leading, axis, down)  10 us
    convert_element_type x1, other arithmetic, per_device(): depthwise(padded, w_depth, lat_rows, lon_cols).astype(jnp.bfloat16)  8.65 us
  transfers between devices with their start and end apart: 9, of which 9 were waited for; matrix products, arithmetic and copies ran while one was open for 5% of the time, Pallas kernels for 0%

commit v1 on v0

v1 whole, which is shorter than its diff:
```python
import functools

import jax
import jax.numpy as jnp
from jax import lax
from jax.experimental import pallas as pl
from jax.experimental.pallas import tpu as pltpu
from jax.sharding import PartitionSpec as P

C = 1024
KERNEL = 7
REACH = 3
EPS = 1e-06
IN_ROWS = 128
OUT_ROWS = 64
BF = jnp.bfloat16
F32 = jnp.float32


def div(a, b):
    return lax.div(a, jnp.int32(b))


def mod(a, b):
    return lax.rem(a, jnp.int32(b))


def home_device(x, y, z, core):
    return (mod(z, 3) * 4 + x) * 2 + core, y * 4 + div(z, 3)


def work_device(low, half, x, sector):
    y, high = div(sector, 4), mod(sector, 4)
    z = mod(13 - 2 * (2 * low + half) + mod(div(high, 2) + y, 2), 12)
    return home_device(x, y, z, mod(high, 2))


def remote(src, dst, sends, recvs, device):
    return pltpu.make_async_remote_copy(
        src_ref=src,
        dst_ref=dst,
        send_sem=sends,
        recv_sem=recvs,
        device_id=device,
        device_id_type=pl.DeviceIdType.MESH,
    )


def kernel(
    f_ref, gain_conv, w_depth, w_ref, gain_attn, gain_out, out_ref,
    wbuf, pad, normed, lat_in, strip32, strip16, lon_in, conv, mixed, moved_out, moved_in,
    qz, kv, attended, back_out, back_in,
    own_sem, wz_s, wz_r, wx_s, wx_r, wc_s, wc_r, lat_s, lat_r, lon_s, lon_r,
    in_s, in_r, kv_s, kv_r, back_s, back_r,
):
    lat, lon = lax.axis_index("lat"), lax.axis_index("lon")
    core, x, low = mod(lat, 2), mod(div(lat, 2), 4), div(lat, 8)
    y, high = div(lon, 4), mod(lon, 4)
    z = high * 3 + low
    z_next = home_device(x, y, mod(z + 1, 12), core)
    z_prev = home_device(x, y, mod(z + 11, 12), core)
    x_next = ((low * 4 + mod(x + 1, 4)) * 2 + core, lon)
    x_prev = ((low * 4 + mod(x + 3, 4)) * 2 + core, lon)
    partner = (lat + 1 - 2 * core, lon)
    lat_next, lat_prev = (mod(lat + 1, 24), lon), (mod(lat + 23, 24), lon)
    lon_next, lon_prev = (lat, mod(lon + 1, 32)), (lat, mod(lon + 31, 32))
    slot = mod(z + 11, 12)
    pair = mod(6 - div(slot, 2), 6)
    part = mod(mod(slot, 2) + y, 2)
    r_low, r_half = div(pair, 2), mod(pair, 2)
    r_sector = y * 4 + 2 * part + core
    origin = ((r_low * 4 + x) * 2 + r_half, r_sector)
    target = work_device(low, core, x, lon)
    outward = 1 - 2 * core
    near = work_device(r_low, r_half, x, mod(r_sector - outward + 32, 32))
    far = work_device(r_low, r_half, x, mod(r_sector + 2 * outward + 32, 32))
    far_from = work_device(r_low, r_half, x, mod(r_sector - 2 * outward + 32, 32))

    barrier = pltpu.get_barrier_semaphore()
    greeted = (
        z_next, z_prev, x_next, x_prev, partner, lat_next, lat_prev, lon_next, lon_prev,
        origin, target, near, far_from,
    )
    for device in greeted:
        pl.semaphore_signal(
            barrier, inc=1, device_id=device, device_id_type=pl.DeviceIdType.MESH
        )
    pl.semaphore_wait(barrier, len(greeted))

    sent = []

    def go(copy):
        copy.start()
        sent.append(copy)
        return copy

    def block(lo, column):
        return (lo * 4 + mod(column + 4, 4)) * 2 + core

    def wx(lo, way, src=None):
        if way < 2:
            b = block(lo, x)
            source, dst = wbuf.at[b], wbuf.at[b]
        else:
            b = block(lo, x - 1 if way == 2 else x + 1)
            rows = pl.ds(0 if way == 2 else C // 2, C // 2)
            source, dst = wbuf.at[b, rows], wbuf.at[b, rows]
        device = x_next if way % 2 == 0 else x_prev
        return remote(src if src is not None else source, dst, wx_s.at[lo, way], wx_r.at[lo, way], device)

    def wc(lo, step, src=None):
        b = block(lo, x + (0, -1, 1, 2)[step])
        return remote(src if src is not None else wbuf.at[b], wbuf.at[b], wc_s.at[lo, step], wc_r.at[lo, step], partner)

    keep = pltpu.make_async_copy(w_ref, wbuf.at[lat], own_sem)
    keep.start()
    to_next = go(remote(w_ref, wbuf.at[lat], wz_s.at[0], wz_r.at[0], z_next))
    to_prev = go(remote(w_ref, wbuf.at[lat], wz_s.at[1], wz_r.at[1], z_prev))
    go(wx(low, 0, w_ref))
    go(wx(low, 1, w_ref))
    go(wc(low, 0, w_ref))

    def spread(lo):
        go(wx(lo, 0))
        go(wx(lo, 1))
        go(wc(lo, 0))

    def pass_on(lo):
        wx(lo, 0).wait_recv()
        go(wx(lo, 2))
        go(wc(lo, 1))
        wx(lo, 1).wait_recv()
        go(wx(lo, 3))
        go(wc(lo, 2))

    def finish(lo):
        wx(lo, 2).wait_recv()
        wx(lo, 3).wait_recv()
        go(wc(lo, 3))

    def arrived(lo):
        for step in range(4):
            wc(lo, step).wait_recv()

    gain = gain_conv[...]

    def norm_row(row, carry):
        value = f_ref[row].astype(F32)
        mean = jnp.mean(value * value, axis=-1, keepdims=True)
        value = (value * lax.rsqrt(mean + EPS) * gain).astype(BF)
        normed[row] = value
        wide = value.astype(F32)
        for k in range(8):
            pad[k, row + REACH, REACH : REACH + 16, :] = wide[:, k * 128 : (k + 1) * 128]
        return carry

    lax.fori_loop(0, 16, norm_row, 0)

    down = remote(normed.at[pl.ds(13, 3)], lat_in.at[0], lat_s.at[0], lat_r.at[0], lat_next)
    up = remote(normed.at[pl.ds(0, 3)], lat_in.at[1], lat_s.at[1], lat_r.at[1], lat_prev)

    @pl.when(lat < 23)
    def _():
        down.start()

    @pl.when(lat > 0)
    def _():
        up.start()

    for side, here, base in ((0, lat > 0, 0), (1, lat < 23, 19)):
        copy = down if side == 0 else up

        @pl.when(here)
        def _():
            copy.wait_recv()
            for row in range(3):
                wide = lat_in[side, row].astype(F32)
                for k in range(8):
                    pad[k, base + row, REACH : REACH + 16, :] = wide[:, k * 128 : (k + 1) * 128]

        @pl.when(jnp.logical_not(here))
        def _():
            for row in range(3):
                for k in range(8):
                    pad[k, base + row, REACH : REACH + 16, :] = jnp.zeros((16, 128), F32)

    strip32[pl.ds(64, 16), :] = jnp.zeros((16, C), F32)
    lon_copies = []
    for side, first, device in ((0, 16, lon_next), (1, REACH, lon_prev)):
        for row in range(22):
            for k in range(8):
                strip32[pl.ds(row * 3, 3), k * 128 : (k + 1) * 128] = pad[k, row, first : first + 3, :]
        strip16[side] = strip32[...].astype(BF)
        lon_copies.append(go(remote(strip16.at[side], lon_in.at[side], lon_s.at[side], lon_r.at[side], device)))

    keep.wait()
    to_next.wait_recv()
    to_prev.wait_recv()
    spread(mod(low + 1, 3))
    spread(mod(low + 2, 3))
    pass_on(0)

    for side, first in ((0, 0), (1, 19)):
        lon_copies[side].wait_recv()
        strip32[...] = lon_in[side].astype(F32)
        for row in range(22):
            for k in range(8):
                pad[k, row, first : first + 3, :] = strip32[pl.ds(row * 3, 3), k * 128 : (k + 1) * 128]

    def depthwise(top):
        def lanes(k, carry):
            at = pl.multiple_of(k * 128, 128)
            total = [None] * 8
            for b in range(KERNEL):
                for row in range(8 + 2 * REACH):
                    value = pad[k, top + row, b : b + 16, :]
                    for a in range(KERNEL):
                        i = row - a
                        if 0 <= i < 8:
                            term = value * w_depth[a, b : b + 1, pl.ds(at, 128)]
                            total[i] = term if total[i] is None else total[i] + term
            for i in range(8):
                conv[pl.ds((top + i) * 16, 16), pl.ds(at, 128)] = total[i].astype(BF)
            return carry

        lax.fori_loop(0, 8, lanes, 0)

    def weights(n):
        return jnp.concatenate([wbuf[2 * n], wbuf[2 * n + 1]], axis=1)

    def pointwise(start):
        rows = pl.ds(start, IN_ROWS)
        value = conv[rows, :]

        def columns(n, carry):
            at = pl.ds(pl.multiple_of(n * 256, 256), 256)
            own = f_ref[pl.ds(start // 16, IN_ROWS // 16), :, at].reshape(IN_ROWS, 256)
            mixed[rows, at] = own.astype(F32) + jnp.dot(value, weights(n), preferred_element_type=F32)
            return carry

        lax.fori_loop(0, 4, columns, 0)

    attn_gain = gain_attn[...]

    def attn_norm(start):
        def some(n, carry):
            rows = pl.ds(pl.multiple_of(start + n * 32, 32), 32)
            value = mixed[rows, :]
            mean = jnp.mean(value * value, axis=-1, keepdims=True)
            moved_out[rows, :] = (value * lax.rsqrt(mean + EPS) * attn_gain).astype(BF)
            return carry

        lax.fori_loop(0, IN_ROWS // 32, some, 0)

    depthwise(0)
    finish(0)
    pass_on(2)
    arrived(0)
    moves = []
    for i in range(256 // IN_ROWS):
        if i:
            depthwise(i * IN_ROWS // 16)
        pointwise(i * IN_ROWS)
        attn_norm(i * IN_ROWS)
        rows = pl.ds(i * IN_ROWS, IN_ROWS)
        moves.append(go(remote(moved_out.at[rows], moved_in.at[rows], in_s.at[i], in_r.at[i], target)))

    finish(2)
    pass_on(1)
    arrived(2)

    pieces = []
    for i in range(256 // IN_ROWS):
        rows = pl.ds(i * IN_ROWS, IN_ROWS)
        moves[i].wait_recv()
        value = moved_in[rows, :]

        def columns(n, carry):
            at = pl.ds(pl.multiple_of(n * 256, 256), 256)
            kv[0, rows, at] = jnp.dot(value, weights(n + 8), preferred_element_type=F32).astype(BF)
            return carry

        lax.fori_loop(0, 4, columns, 0)
        pieces.append(
            [
                go(remote(kv.at[0, rows], kv.at[to, rows], kv_s.at[i, to], kv_r.at[i, to], device))
                for to, device in ((3, near), (2, far), (1, partner))
            ]
        )

    finish(1)
    arrived(1)

    left_half = lax.broadcasted_iota(jnp.int32, (256, 128), 1) < 64

    def queries(i, carry):
        value = jnp.dot(moved_in[...], weights(i + 4), preferred_element_type=F32)
        value = value.astype(BF).astype(F32) * 0.125
        first, second = value[:, :128], value[:, 128:]
        zero = jnp.zeros_like(first)
        qz[i, 0] = jnp.where(left_half, first, zero).astype(BF)
        qz[i, 1] = jnp.where(left_half, pltpu.roll(first, 64, 1), zero).astype(BF)
        qz[i, 2] = jnp.where(left_half, zero, pltpu.roll(second, 64, 1)).astype(BF)
        qz[i, 3] = jnp.where(left_half, zero, second).astype(BF)
        return carry

    lax.fori_loop(0, 4, queries, 0)

    for i, (to_near, to_far, to_partner) in enumerate(pieces):
        rows = pl.ds(i * IN_ROWS, IN_ROWS)
        to_near.wait_recv()
        to_near = go(remote(kv.at[3, rows], kv.at[4, rows], kv_s.at[i, 4], kv_r.at[i, 4], partner))
        pieces[i].append(to_near)
    for _, to_far, to_partner, relayed in pieces:
        to_far.wait_recv()
        to_partner.wait_recv()
        relayed.wait_recv()

    out_gain = gain_out[...]
    half = lax.broadcasted_iota(jnp.int32, (OUT_ROWS, 128), 1) < 64

    def attend(start):
        rows = pl.ds(start, OUT_ROWS)

        def heads(i, carry):
            at = pl.ds(pl.multiple_of(i * 128, 128), 128)
            values_at = pl.ds(pl.multiple_of(i * 128 + C // 2, 128), 128)
            query = qz[i, :, rows, :].reshape(4 * OUT_ROWS, 128)
            keys = kv[:, :, at].reshape(1280, 128)
            values = kv[:, :, values_at].reshape(1280, 128)
            scores = lax.dot_general(query, keys, (((1,), (1,)), ((), ())), preferred_element_type=F32)
            peak = jnp.max(scores, axis=-1, keepdims=True)
            expo = jnp.exp(scores - peak).astype(BF)
            wide = jnp.concatenate([values, jnp.ones((1280, 128), BF)], axis=1)
            both = jnp.dot(expo, wide, preferred_element_type=F32)
            result = (both[:, :128] / both[:, 128:]).reshape(4, OUT_ROWS, 128)
            first = jnp.where(half, result[0], pltpu.roll(result[1], 64, 1))
            second = jnp.where(half, pltpu.roll(result[2], 64, 1), result[3])
            out_at = pl.multiple_of(i * 256, 256)
            attended[:, pl.ds(out_at, 128)] = first
            attended[:, pl.ds(out_at + 128, 128)] = second
            return carry

        lax.fori_loop(0, 4, heads, 0)
        value = attended[...]
        mean = jnp.mean(value * value, axis=-1, keepdims=True)
        back_out[rows, :] = (value * lax.rsqrt(mean + EPS) * out_gain).astype(BF)

    backs = []
    for i in range(256 // OUT_ROWS):
        attend(i * OUT_ROWS)
        rows = pl.ds(i * OUT_ROWS, OUT_ROWS)
        backs.append(go(remote(back_out.at[rows], back_in.at[rows], back_s.at[i], back_r.at[i], origin)))
    for i, copy in enumerate(backs):
        rows = pl.ds(i * OUT_ROWS, OUT_ROWS)
        copy.wait_recv()
        total = mixed[rows, :] + back_in[rows, :].astype(F32)
        out_ref[pl.ds(i * OUT_ROWS // 16, OUT_ROWS // 16)] = total.astype(BF).reshape(OUT_ROWS // 16, 16, C)

    for copy in sent:
        copy.wait_send()

    @pl.when(lat < 23)
    def _():
        down.wait_send()

    @pl.when(lat > 0)
    def _():
        up.wait_send()


def per_device(fields, gain_conv, w_depth, w_layer, gain_attn, gain_out):
    vmem = pl.BlockSpec(memory_space=pltpu.VMEM)
    dma = pltpu.SemaphoreType.DMA
    n_in, n_out = 256 // IN_ROWS, 256 // OUT_ROWS
    return pl.pallas_call(
        kernel,
        out_shape=jax.ShapeDtypeStruct(fields.shape, BF),
        in_specs=[vmem, vmem, vmem, pl.BlockSpec(memory_space=pl.ANY), vmem, vmem],
        out_specs=vmem,
        scratch_shapes=[
            pltpu.VMEM((24, C, 128), BF),
            pltpu.VMEM((8, 22, 24, 128), F32),
            pltpu.VMEM((16, 16, C), BF),
            pltpu.VMEM((2, 3, 16, C), BF),
            pltpu.VMEM((80, C), F32),
            pltpu.VMEM((2, 80, C), BF),
            pltpu.VMEM((2, 80, C), BF),
            pltpu.VMEM((256, C), BF),
            pltpu.VMEM((256, C), F32),
            pltpu.VMEM((256, C), BF),
            pltpu.VMEM((256, C), BF),
            pltpu.VMEM((4, 4, 256, 128), BF),
            pltpu.VMEM((5, 256, C), BF),
            pltpu.VMEM((OUT_ROWS, C), F32),
            pltpu.VMEM((256, C), BF),
            pltpu.VMEM((256, C), BF),
            dma,
            dma((2,)), dma((2,)),
            dma((3, 4)), dma((3, 4)),
            dma((3, 4)), dma((3, 4)),
            dma((2,)), dma((2,)),
            dma((2,)), dma((2,)),
            dma((n_in,)), dma((n_in,)),
            dma((n_in, 5)), dma((n_in, 5)),
            dma((n_out,)), dma((n_out,)),
        ],
        compiler_params=pltpu.CompilerParams(
            collective_id=0, has_side_effects=True, vmem_limit_bytes=60 * 1024 * 1024
        ),
        name="layer",
    )(
        fields, gain_conv.reshape(1, C), w_depth, w_layer,
        gain_attn.reshape(1, C), gain_out.reshape(1, C),
    )


def solution(mesh):
    return jax.shard_map(
        per_device,
        mesh=mesh,
        in_specs=(P("lat", "lon", None), P(), P(), P(None, "lat"), P(), P()),
        out_specs=P("lat", "lon", None),
        check_vma=False,
    )
```

time: 303 us -> 111 us (0.37)
  the two profiles are of different devices: /device:TPU:76 before, /device:TPU:1 now
where the time goes in v1:
time: 111 us
  Pallas kernels  109 us (98%)
  local copies, waits for them, and re-layouts  1.88 us (2%)
    pallas_call x1, Pallas kernels, per_device(): pl.pallas_call(kernel, out_shape=jax.ShapeDtypeStruct(fields.shape, BF),...  109 us

profile of v1, /device:TPU:1, one launch (start us, length us, event | category | flops | bytes accessed | tf_op | source)
XLA Modules:
  0.0 111.0 jit_solution(1848854255380180260)
XLA Ops:
  0.0 109.1 %layer.1 = bf16[16,16,1024]{2,1,0:T(8,128)(2,1)} custom-call(bf16[16,16,1024]{2,1,0:T(8,128)(2,1)} %f_ref.1, f32[1,1024]{1,0:T(1,128)} %bitcast.3, f32[7,7,1024]{2,1,0:T(8,128)} %w_depth.1, bf16[1024,128]{1,0:T(8,128)(2,1)} %w_ref.1, f32[1,1024]{1,0:T(1,128)} %bitcast.4, f32[1,1024]{1,0:T(1,128)} %bitcast.5), custom_call_target="tpu_custom_call" | custom-call | tf_op jit(solution)/shard_map/layer/pallas_call | solution.py:376
  109.1 1.9 %copy.8 = bf16[16,16,1024]{2,1,0:T(8,128)(2,1)} copy(bf16[16,16,1024]{2,1,0:T(8,128)(2,1)} %layer.1) | data formatting | bytes 1048576

commit v2 on v1

v2 whole, which is shorter than its diff:
```python
import functools

import jax
import jax.numpy as jnp
from jax import lax
from jax.experimental import pallas as pl
from jax.experimental.pallas import tpu as pltpu
from jax.sharding import PartitionSpec as P

C = 1024
KERNEL = 7
REACH = 3
EPS = 1e-06
MIX_ROWS = 128
IN_ROWS = 64
OUT_ROWS = (32, 32, 64, 64, 64)
BF = jnp.bfloat16
F32 = jnp.float32


def div(a, b):
    return lax.div(a, jnp.int32(b))


def mod(a, b):
    return lax.rem(a, jnp.int32(b))


def home_device(x, y, z, core):
    return (mod(z, 3) * 4 + x) * 2 + core, y * 4 + div(z, 3)


BAND_Z = (10, 7, 11, 5, 8, 2, 3, 9, 1, 4, 6, 0)
BAND_FLIP = (0, 0, 1, 1, 1, 0, 0, 0, 1, 1, 0, 0)


def pick(table, index):
    value = jnp.int32(0)
    for i, entry in enumerate(table):
        if entry:
            value = value + jnp.where(index == i, jnp.int32(entry), jnp.int32(0))
    return value


def work_device(band, x_pair, sector):
    y, high = div(sector, 4), mod(sector, 4)
    x = 2 * x_pair + mod(div(high, 2) + y + pick(BAND_FLIP, band), 2)
    return home_device(x, y, pick(BAND_Z, band), mod(high, 2))


def remote(src, dst, sends, recvs, device):
    return pltpu.make_async_remote_copy(
        src_ref=src,
        dst_ref=dst,
        send_sem=sends,
        recv_sem=recvs,
        device_id=device,
        device_id_type=pl.DeviceIdType.MESH,
    )


def kernel(
    f_ref, gain_conv, w_depth, w_ref, gain_attn, gain_out, mixed, back_in,
    wbuf, pad, edge, inner, normed, lat_in, strip32, strip16, lon_in, corner_out, corner_in, conv, moved_out, moved_in,
    qz, kv, attended, back_out,
    own_sem, wz_s, wz_r, wx_s, wx_r, wy_s, wy_r, wc_s, wc_r, lat_s, lat_r, lon_s, lon_r, corner_s, corner_r,
    in_s, in_r, kv_s, kv_r, back_s, back_r,
):
    lat, lon = lax.axis_index("lat"), lax.axis_index("lon")
    core, x, low = mod(lat, 2), mod(div(lat, 2), 4), div(lat, 8)
    y, high = div(lon, 4), mod(lon, 4)
    z = high * 3 + low
    z_next = home_device(x, y, mod(z + 1, 12), core)
    z_prev = home_device(x, y, mod(z + 11, 12), core)
    x_next = ((low * 4 + mod(x + 1, 4)) * 2 + core, lon)
    x_prev = ((low * 4 + mod(x + 3, 4)) * 2 + core, lon)
    partner = (lat + 1 - 2 * core, lon)
    lat_next, lat_prev = (mod(lat + 1, 24), lon), (mod(lat + 23, 24), lon)
    lon_next, lon_prev = (lat, mod(lon + 1, 32)), (lat, mod(lon + 31, 32))
    y_next, y_prev = (lat, mod(lon + 4, 32)), (lat, mod(lon + 28, 32))
    x_pair = div(x, 2)
    band = pick([BAND_Z.index(i) for i in range(12)], z)
    part = mod(mod(x, 2) + y + pick(BAND_FLIP, band), 2)
    sector = y * 4 + 2 * part + core
    origin = ((div(band, 4) * 4 + 2 * x_pair + mod(div(band, 2), 2)) * 2 + mod(band, 2), sector)
    target = work_device(low * 4 + mod(x, 2) * 2 + core, x_pair, lon)
    outward = 1 - 2 * core
    near = work_device(band, x_pair, mod(sector - outward + 32, 32))
    far = work_device(band, x_pair, mod(sector + 2 * outward + 32, 32))
    far_from = work_device(band, x_pair, mod(sector - 2 * outward + 32, 32))

    barrier = pltpu.get_barrier_semaphore()
    greeted = (
        z_next, z_prev, x_next, x_prev, y_next, y_prev, partner, lat_next, lat_prev, lon_next, lon_prev,
        origin, target, near, far_from,
    )
    for device in greeted:
        pl.semaphore_signal(
            barrier, inc=1, device_id=device, device_id_type=pl.DeviceIdType.MESH
        )

    def clear(row, carry):
        zero = jnp.zeros((8, 128), F32)
        for k in range(8):
            for first in (0, 16):
                pad[k, row, first : first + 8, :] = zero
            for side in range(2):
                for first in (0, 8):
                    edge[side, k, row, first : first + 8, :] = zero
        return carry

    lax.fori_loop(0, 22, clear, 0)
    pl.semaphore_wait(barrier, len(greeted))

    sent = []

    def go(copy):
        copy.start()
        sent.append(copy)
        return copy

    HALF, QUARTER = C // 2, C // 4
    mine = pl.multiple_of(mod(y, 2) * HALF, HALF)

    def block(lo, step):
        return (lo * 4 + mod(x + (0, 3, 1, 2)[step], 4)) * 2 + core

    def wx(lo, way, src=None):
        b = block(lo, (0, 0, 1, 2)[way])
        rows = (pl.ds(mine, HALF), pl.ds(mine, HALF), pl.ds(mine, QUARTER), pl.ds(mine + QUARTER, QUARTER))[way]
        piece = wbuf.at[b, rows]
        source = piece if src is None else src.at[rows]
        return remote(source, piece, wx_s.at[lo, way], wx_r.at[lo, way], x_prev if way % 2 else x_next)

    def wy(lo, step, way):
        piece = wbuf.at[block(lo, step), pl.ds(mine + way * QUARTER, QUARTER)]
        at = step * 2 + way
        return remote(piece, piece, wy_s.at[lo, at], wy_r.at[lo, at], y_next if way else y_prev)

    def wc(lo, step, src=None):
        piece = wbuf.at[block(lo, step)]
        return remote(piece if src is None else src, piece, wc_s.at[lo, step], wc_r.at[lo, step], partner)

    keep = pltpu.make_async_copy(w_ref, wbuf.at[lat], own_sem)
    keep.start()
    own_half, there = w_ref.at[pl.ds(mine, HALF)], wbuf.at[lat, pl.ds(mine, HALF)]
    go(remote(own_half, there, wz_s.at[0], wz_r.at[0], z_next))
    go(remote(own_half, there, wz_s.at[1], wz_r.at[1], z_prev))
    for copy in (wx(low, 0, w_ref), wx(low, 1, w_ref), wc(low, 0, w_ref)):
        copy.start()
    for lo in range(3):
        sent.extend((wx(lo, 0), wx(lo, 1), wc(lo, 0)))

    def spread(lo):
        @pl.when(low != lo)
        def _():
            side = 2 - mod(lo - low + 3, 3)
            here = wbuf.at[block(lo, 0), pl.ds(mine, HALF)]
            remote(own_half, here, wz_s.at[0], wz_r.at[side], z_next).wait_recv()
            for copy in (wx(lo, 0), wx(lo, 1), wy(lo, 0, 0), wy(lo, 0, 1)):
                copy.start()

    def pass_on(lo):
        for way in range(2):
            wx(lo, way).wait_recv()
            go(wx(lo, 2 + way))
            go(wy(lo, 1 + way, 0))
            go(wy(lo, 1 + way, 1))

    def relay(lo):
        wx(lo, 2).wait_recv()
        wx(lo, 3).wait_recv()
        go(wy(lo, 3, 0))
        go(wy(lo, 3, 1))

    def finish(lo):
        @pl.when(low != lo)
        def _():
            wy(lo, 0, 0).wait_recv()
            wy(lo, 0, 1).wait_recv()
            wc(lo, 0).start()

        for step in range(1, 4):
            wy(lo, step, 0).wait_recv()
            wy(lo, step, 1).wait_recv()
            go(wc(lo, step))

    def arrived(lo):
        for step in range(4):
            wc(lo, step).wait_recv()

    gain = gain_conv[...]

    def norm_row(row, carry):
        value = f_ref[row].astype(F32)
        mean = jnp.mean(value * value, axis=-1, keepdims=True)
        value = (value * lax.rsqrt(mean + EPS) * gain).astype(BF)
        normed[row] = value
        wide = value.astype(F32)
        for k in range(8):
            pad[k, row + REACH, REACH : REACH + 16, :] = wide[:, k * 128 : (k + 1) * 128]
        return carry

    lax.fori_loop(0, 16, norm_row, 0)

    down = remote(normed.at[pl.ds(13, 3)], lat_in.at[0], lat_s.at[0], lat_r.at[0], lat_next)
    up = remote(normed.at[pl.ds(0, 3)], lat_in.at[1], lat_s.at[1], lat_r.at[1], lat_prev)

    @pl.when(lat < 23)
    def _():
        down.start()

    @pl.when(lat > 0)
    def _():
        up.start()

    sides = ((0, 16, lon_next), (1, REACH, lon_prev))
    lon_copies, corner_copies = [], []
    for side, first, device in sides:
        for row in range(16):
            for k in range(8):
                strip32[pl.ds(row * 3, 3), k * 128 : (k + 1) * 128] = pad[k, row + REACH, first : first + 3, :]
        strip16[side] = strip32[...].astype(BF)
        lon_copies.append(go(remote(strip16.at[side], lon_in.at[side], lon_s.at[side], lon_r.at[side], device)))

    for side, here, base in ((0, lat > 0, 0), (1, lat < 23, 19)):
        copy = down if side == 0 else up

        @pl.when(here)
        def _():
            copy.wait_recv()
            for row in range(3):
                wide = lat_in[side, row].astype(F32)
                for k in range(8):
                    pad[k, base + row, REACH : REACH + 16, :] = wide[:, k * 128 : (k + 1) * 128]

        @pl.when(jnp.logical_not(here))
        def _():
            for row in range(3):
                for k in range(8):
                    pad[k, base + row, REACH : REACH + 16, :] = jnp.zeros((16, 128), F32)

    strip32[pl.ds(16, 8), :] = jnp.zeros((8, C), F32)
    for side, first, device in sides:
        for n in range(6):
            row = n if n < 3 else n + 16
            for k in range(8):
                strip32[pl.ds(n * 3, 3), k * 128 : (k + 1) * 128] = pad[k, row, first : first + 3, :]
        corner_out[side] = strip32[pl.ds(0, 24), :].astype(BF)
        corner_copies.append(
            go(remote(corner_out.at[side], corner_in.at[side], corner_s.at[side], corner_r.at[side], device))
        )

    deep = 8

    def depthwise(top):
        def lanes(k, carry):
            at = pl.multiple_of(k * 128, 128)
            total = [None] * deep
            for b in range(KERNEL):
                for row in range(deep + 2 * REACH):
                    value = pad[k, top + row, b : b + 16, :]
                    for a in range(KERNEL):
                        i = row - a
                        if 0 <= i < deep:
                            term = value * w_depth[a, b : b + 1, pl.ds(at, 128)]
                            total[i] = term if total[i] is None else total[i] + term
            for i in range(deep):
                inner[k, top + i] = total[i]
            return carry

        lax.fori_loop(0, 8, lanes, 0)

    def neighbours(top):
        def lanes(k, carry):
            at = pl.multiple_of(k * 128, 128)
            total = [[inner[k, top + i, side * 8 : side * 8 + 8, :] for i in range(deep)] for side in range(2)]
            for side in range(2):
                for shift in range(REACH):
                    b = shift + 4 * side
                    for row in range(deep + 2 * REACH):
                        value = edge[side, k, top + row, shift : shift + 8, :]
                        for a in range(KERNEL):
                            i = row - a
                            if 0 <= i < deep:
                                total[side][i] += value * w_depth[a, b : b + 1, pl.ds(at, 128)]
            for i in range(deep):
                both = jnp.concatenate([total[0][i], total[1][i]], axis=0)
                conv[pl.ds((top + i) * 16, 16), pl.ds(at, 128)] = both.astype(BF)
            return carry

        lax.fori_loop(0, 8, lanes, 0)

    def weights(n):
        return jnp.concatenate([wbuf[2 * n], wbuf[2 * n + 1]], axis=1)

    def pointwise(start):
        rows = pl.ds(start, MIX_ROWS)
        value = conv[rows, :]

        def columns(n, carry):
            at = pl.ds(pl.multiple_of(n * 256, 256), 256)
            own = f_ref[pl.ds(start // 16, MIX_ROWS // 16), :, at].reshape(MIX_ROWS, 256)
            mixed[rows, at] = own.astype(F32) + jnp.dot(value, weights(n), preferred_element_type=F32)
            return carry

        lax.fori_loop(0, 4, columns, 0)

    attn_gain = gain_attn[...]

    def attn_norm(start):
        def some(n, carry):
            rows = pl.ds(pl.multiple_of(start + n * 32, 32), 32)
            value = mixed[rows, :]
            mean = jnp.mean(value * value, axis=-1, keepdims=True)
            moved_out[rows, :] = (value * lax.rsqrt(mean + EPS) * attn_gain).astype(BF)
            return carry

        lax.fori_loop(0, IN_ROWS // 32, some, 0)

    spread(0)
    depthwise(0)
    pass_on(0)
    depthwise(deep)
    spread(2)
    spread(1)
    relay(0)
    keep.wait()
    for side, first in ((0, 0), (1, 7)):
        lon_copies[side].wait_recv()
        strip32[...] = lon_in[side].astype(F32)
        for row in range(16):
            for k in range(8):
                edge[side, k, row + REACH, first : first + 3, :] = strip32[pl.ds(row * 3, 3), k * 128 : (k + 1) * 128]
    for side, first in ((0, 0), (1, 7)):
        corner_copies[side].wait_recv()
        strip32[pl.ds(0, 24), :] = corner_in[side].astype(F32)
        for n in range(6):
            row = n if n < 3 else n + 16
            for k in range(8):
                edge[side, k, row, first : first + 3, :] = strip32[pl.ds(n * 3, 3), k * 128 : (k + 1) * 128]
    neighbours(0)
    finish(0)
    neighbours(deep)
    pass_on(2)
    relay(2)
    arrived(0)
    moves = []
    for i in range(256 // MIX_ROWS):
        pointwise(i * MIX_ROWS)
        for j in range(i * MIX_ROWS // IN_ROWS, (i + 1) * MIX_ROWS // IN_ROWS):
            attn_norm(j * IN_ROWS)
            rows = pl.ds(j * IN_ROWS, IN_ROWS)
            moves.append(go(remote(moved_out.at[rows], moved_in.at[rows], in_s.at[j], in_r.at[j], target)))

    finish(2)
    pass_on(1)
    relay(1)
    arrived(2)

    pieces = []
    for i in range(256 // IN_ROWS):
        rows = pl.ds(i * IN_ROWS, IN_ROWS)
        moves[i].wait_recv()
        value = moved_in[rows, :]

        def columns(n, carry):
            at = pl.ds(pl.multiple_of(n * 256, 256), 256)
            kv[0, rows, at] = jnp.dot(value, weights(n + 8), preferred_element_type=F32).astype(BF)
            return carry

        lax.fori_loop(0, 4, columns, 0)
        pieces.append(
            [
                go(remote(kv.at[0, rows], kv.at[to, rows], kv_s.at[i, to], kv_r.at[i, to], device))
                for to, device in ((3, near), (2, far), (1, partner))
            ]
        )

    finish(1)
    arrived(1)

    left_half = lax.broadcasted_iota(jnp.int32, (256, 128), 1) < 64

    def queries(i, carry):
        value = jnp.dot(moved_in[...], weights(i + 4), preferred_element_type=F32)
        value = value.astype(BF).astype(F32) * 0.125
        first, second = value[:, :128], value[:, 128:]
        zero = jnp.zeros_like(first)
        qz[i, 0] = jnp.where(left_half, first, zero).astype(BF)
        qz[i, 1] = jnp.where(left_half, pltpu.roll(first, 64, 1), zero).astype(BF)
        qz[i, 2] = jnp.where(left_half, zero, pltpu.roll(second, 64, 1)).astype(BF)
        qz[i, 3] = jnp.where(left_half, zero, second).astype(BF)
        return carry

    lax.fori_loop(0, 4, queries, 0)

    for i, (to_near, to_far, to_partner) in enumerate(pieces):
        rows = pl.ds(i * IN_ROWS, IN_ROWS)
        to_near.wait_recv()
        to_near = go(remote(kv.at[3, rows], kv.at[4, rows], kv_s.at[i, 4], kv_r.at[i, 4], partner))
        pieces[i].append(to_near)
    for _, to_far, to_partner, relayed in pieces:
        to_far.wait_recv()
        to_partner.wait_recv()
        relayed.wait_recv()

    out_gain = gain_out[...]
    def attend(start, size):
        rows = pl.ds(start, size)
        half = lax.broadcasted_iota(jnp.int32, (size, 128), 1) < 64

        def heads(i, carry):
            at = pl.ds(pl.multiple_of(i * 128, 128), 128)
            values_at = pl.ds(pl.multiple_of(i * 128 + C // 2, 128), 128)
            query = qz[i, :, rows, :].reshape(4 * size, 128)
            keys = kv[:, :, at].reshape(1280, 128)
            values = kv[:, :, values_at].reshape(1280, 128)
            scores = lax.dot_general(query, keys, (((1,), (1,)), ((), ())), preferred_element_type=F32)
            peak = jnp.max(scores, axis=-1, keepdims=True)
            expo = jnp.exp(scores - peak).astype(BF)
            wide = jnp.concatenate([values, jnp.ones((1280, 128), BF)], axis=1)
            both = jnp.dot(expo, wide, preferred_element_type=F32)
            result = (both[:, :128] / both[:, 128:]).reshape(4, size, 128)
            first = jnp.where(half, result[0], pltpu.roll(result[1], 64, 1))
            second = jnp.where(half, pltpu.roll(result[2], 64, 1), result[3])
            out_at = pl.multiple_of(i * 256, 256)
            attended[pl.ds(0, size), pl.ds(out_at, 128)] = first
            attended[pl.ds(0, size), pl.ds(out_at + 128, 128)] = second
            return carry

        lax.fori_loop(0, 4, heads, 0)
        value = attended[pl.ds(0, size), :]
        mean = jnp.mean(value * value, axis=-1, keepdims=True)
        back_out[rows, :] = (value * lax.rsqrt(mean + EPS) * out_gain).astype(BF)

    backs, start = [], 0
    for i, size in enumerate(OUT_ROWS):
        attend(start, size)
        rows = pl.ds(start, size)
        backs.append(go(remote(back_out.at[rows], back_in.at[rows], back_s.at[i], back_r.at[i], origin)))
        start += size
    for copy in backs:
        copy.wait_recv()

    for copy in sent:
        copy.wait_send()
    for lo in range(3):

        @pl.when(low != lo)
        def _():
            wy(lo, 0, 0).wait_send()
            wy(lo, 0, 1).wait_send()

    @pl.when(lat < 23)
    def _():
        down.wait_send()

    @pl.when(lat > 0)
    def _():
        up.wait_send()


def per_device(fields, gain_conv, w_depth, w_layer, gain_attn, gain_out):
    vmem = pl.BlockSpec(memory_space=pltpu.VMEM)
    dma = pltpu.SemaphoreType.DMA
    n_in, n_out = 256 // IN_ROWS, len(OUT_ROWS)
    mixed, back = pl.pallas_call(
        kernel,
        out_shape=[jax.ShapeDtypeStruct((256, C), F32), jax.ShapeDtypeStruct((256, C), BF)],
        in_specs=[vmem, vmem, vmem, pl.BlockSpec(memory_space=pl.ANY), vmem, vmem],
        out_specs=[vmem, vmem],
        scratch_shapes=[
            pltpu.VMEM((24, C, 128), BF),
            pltpu.VMEM((8, 22, 24, 128), F32),
            pltpu.VMEM((2, 8, 22, 16, 128), F32),
            pltpu.VMEM((8, 16, 16, 128), F32),
            pltpu.VMEM((16, 16, C), BF),
            pltpu.VMEM((2, 3, 16, C), BF),
            pltpu.VMEM((48, C), F32),
            pltpu.VMEM((2, 48, C), BF),
            pltpu.VMEM((2, 48, C), BF),
            pltpu.VMEM((2, 24, C), BF),
            pltpu.VMEM((2, 24, C), BF),
            pltpu.VMEM((256, C), BF),
            pltpu.VMEM((256, C), BF),
            pltpu.VMEM((256, C), BF),
            pltpu.VMEM((4, 4, 256, 128), BF),
            pltpu.VMEM((5, 256, C), BF),
            pltpu.VMEM((max(OUT_ROWS), C), F32),
            pltpu.VMEM((256, C), BF),
            dma,
            dma((2,)), dma((2,)),
            dma((3, 4)), dma((3, 4)),
            dma((3, 8)), dma((3, 8)),
            dma((3, 4)), dma((3, 4)),
            dma((2,)), dma((2,)),
            dma((2,)), dma((2,)),
            dma((2,)), dma((2,)),
            dma((n_in,)), dma((n_in,)),
            dma((n_in, 5)), dma((n_in, 5)),
            dma((n_out,)), dma((n_out,)),
        ],
        compiler_params=pltpu.CompilerParams(
            collective_id=0, has_side_effects=True, vmem_limit_bytes=60 * 1024 * 1024
        ),
        name="layer",
    )(
        fields, gain_conv.reshape(1, C), w_depth, w_layer,
        gain_attn.reshape(1, C), gain_out.reshape(1, C),
    )
    return (mixed + back.astype(F32)).astype(BF).reshape(fields.shape)


def solution(mesh):
    return jax.shard_map(
        per_device,
        mesh=mesh,
        in_specs=(P("lat", "lon", None), P(), P(), P(None, "lat"), P(), P()),
        out_specs=P("lat", "lon", None),
        check_vma=False,
    )
```

time: 111 us -> 113 us (1.018)
  other arithmetic: 0 us -> 2.3 us
  local copies, waits for them, and re-layouts: 1.88 us -> 0 us
    convert_element_type x0 -> x1, other arithmetic: none -> 2.3 us  [per_device(): return (mixed + back.astype(F32)).astype(BF).reshape(fields.shape)]
    unnamed x1 -> x0, local copies, waits for them, and re-layouts: 1.88 us -> none
where the time goes in v2:
time: 113 us
  Pallas kernels  110 us (97%)
  other arithmetic  2.3 us (2%)
    pallas_call x1, Pallas kernels, per_device(): pl.pallas_call(kernel, out_shape=[jax.ShapeDtypeStruct((256, C), F32), ja...  110 us
    convert_element_type x1, other arithmetic, per_device(): return (mixed + back.astype(F32)).astype(BF).reshape(fields.shape)  2.3 us

profile of v2, /device:TPU:1, one launch (start us, length us, event | category | flops | bytes accessed | tf_op | source)
XLA Modules:
  0.0 112.6 jit_solution(9505487431049666424)
XLA Ops:
  0.0 110.3 %layer.1 = (f32[256,1024]{1,0:T(8,128)}, bf16[256,1024]{1,0:T(8,128)(2,1)}) custom-call(bf16[16,16,1024]{2,1,0:T(8,128)(2,1)} %f_ref.1, f32[1,1024]{1,0:T(1,128)} %bitcast.4, f32[7,7,1024]{2,1,0:T(8,128)} %w_depth.1, bf16[1024,128]{1,0:T(8,128)(2,1)} %w_ref.1, f32[1,1024]{1,0:T(1,128)} %bitcast.5, f32[1,1024]{1,0:T(1,128)} %bitcast.6), custom_call_target="tpu_custom_call" | custom-call | tf_op jit(solution)/shard_map/layer/pallas_call | solution.py:468
  110.3 2.3 %add_convert_fusion = bf16[256,1024]{1,0:T(8,128)(2,1)} fusion(f32[256,1024]{1,0:T(8,128)} %get-tuple-element.7, bf16[256,1024]{1,0:T(8,128)(2,1)} %get-tuple-element.8), kind=kLoop, calls=%fused_computation | loop fusion | flops 786432 | bytes 2097152 | tf_op jit(solution)/shard_map/convert_element_type | solution.py:512

commit v3 on v2

--- a/solution.py
+++ b/solution.py
@@ -319,12 +319,13 @@
         lax.fori_loop(0, IN_ROWS // 32, some, 0)
 
     spread(0)
+    spread(2)
+    pass_on(0)
     depthwise(0)
-    pass_on(0)
+    relay(0)
+    spread(1)
     depthwise(deep)
-    spread(2)
-    spread(1)
-    relay(0)
+    finish(0)
     keep.wait()
     for side, first in ((0, 0), (1, 7)):
         lon_copies[side].wait_recv()
@@ -340,10 +341,8 @@
             for k in range(8):
                 edge[side, k, row, first : first + 3, :] = strip32[pl.ds(n * 3, 3), k * 128 : (k + 1) * 128]
     neighbours(0)
-    finish(0)
+    pass_on(2)
     neighbours(deep)
-    pass_on(2)
-    relay(2)
     arrived(0)
     moves = []
     for i in range(256 // MIX_ROWS):
@@ -353,6 +352,7 @@
             rows = pl.ds(j * IN_ROWS, IN_ROWS)
             moves.append(go(remote(moved_out.at[rows], moved_in.at[rows], in_s.at[j], in_r.at[j], target)))
 
+    relay(2)
     finish(2)
     pass_on(1)
     relay(1)

time: 113 us -> 110 us (0.973)
  Pallas kernels: 110 us -> 108 us
    pallas_call x1, Pallas kernels: 110 us -> 108 us  [per_device(): pl.pallas_call(kernel, out_shape=[jax.ShapeDtypeStruct((256, C), F32), ja...]
where the time goes in v3:
time: 110 us
  Pallas kernels  108 us (98%)
  other arithmetic  2.3 us (2%)
    pallas_call x1, Pallas kernels, per_device(): pl.pallas_call(kernel, out_shape=[jax.ShapeDtypeStruct((256, C), F32), ja...  108 us
    convert_element_type x1, other arithmetic, per_device(): return (mixed + back.astype(F32)).astype(BF).reshape(fields.shape)  2.3 us

profile of v3, /device:TPU:1, one launch (start us, length us, event | category | flops | bytes accessed | tf_op | source)
XLA Modules:
  0.0 110.3 jit_solution(16183408718246322824)
XLA Ops:
  0.0 108.0 %layer.1 = (f32[256,1024]{1,0:T(8,128)}, bf16[256,1024]{1,0:T(8,128)(2,1)}) custom-call(bf16[16,16,1024]{2,1,0:T(8,128)(2,1)} %f_ref.1, f32[1,1024]{1,0:T(1,128)} %bitcast.4, f32[7,7,1024]{2,1,0:T(8,128)} %w_depth.1, bf16[1024,128]{1,0:T(8,128)(2,1)} %w_ref.1, f32[1,1024]{1,0:T(1,128)} %bitcast.5, f32[1,1024]{1,0:T(1,128)} %bitcast.6), custom_call_target="tpu_custom_call" | custom-call | tf_op jit(solution)/shard_map/layer/pallas_call | solution.py:468
  108.0 2.3 %add_convert_fusion = bf16[256,1024]{1,0:T(8,128)(2,1)} fusion(f32[256,1024]{1,0:T(8,128)} %get-tuple-element.7, bf16[256,1024]{1,0:T(8,128)(2,1)} %get-tuple-element.8), kind=kLoop, calls=%fused_computation | loop fusion | flops 786432 | bytes 2097152 | tf_op jit(solution)/shard_map/convert_element_type | solution.py:512

commit v4 on v3

--- a/solution.py
+++ b/solution.py
@@ -377,6 +377,14 @@
             ]
         )
 
+    def hand_over(i):
+        rows = pl.ds(i * IN_ROWS, IN_ROWS)
+        pieces[i][0].wait_recv()
+        pieces[i].append(go(remote(kv.at[3, rows], kv.at[4, rows], kv_s.at[i, 4], kv_r.at[i, 4], partner)))
+
+    for i in range(len(pieces) - 1):
+        hand_over(i)
+
     finish(1)
     arrived(1)
 
@@ -395,11 +403,7 @@
 
     lax.fori_loop(0, 4, queries, 0)
 
-    for i, (to_near, to_far, to_partner) in enumerate(pieces):
-        rows = pl.ds(i * IN_ROWS, IN_ROWS)
-        to_near.wait_recv()
-        to_near = go(remote(kv.at[3, rows], kv.at[4, rows], kv_s.at[i, 4], kv_r.at[i, 4], partner))
-        pieces[i].append(to_near)
+    hand_over(len(pieces) - 1)
     for _, to_far, to_partner, relayed in pieces:
         to_far.wait_recv()
         to_partner.wait_recv()

time: 110 us -> 113 us (1.027)
  Pallas kernels: 108 us -> 110 us
    pallas_call x1, Pallas kernels: 108 us -> 110 us  [per_device(): pl.pallas_call(kernel, out_shape=[jax.ShapeDtypeStruct((256, C), F32), ja...]
where the time goes in v4:
time: 113 us; the launch traced here: 112 us
  Pallas kernels  110 us (97%)
  other arithmetic  2.3 us (2%)
    pallas_call x1, Pallas kernels, per_device(): pl.pallas_call(kernel, out_shape=[jax.ShapeDtypeStruct((256, C), F32), ja...  110 us
    convert_element_type x1, other arithmetic, per_device(): return (mixed + back.astype(F32)).astype(BF).reshape(fields.shape)  2.3 us

profile of v4, /device:TPU:1, one launch (start us, length us, event | category | flops | bytes accessed | tf_op | source)
XLA Modules:
  0.0 112.4 jit_solution(3339155229829091297)
XLA Ops:
  0.0 110.1 %layer.1 = (f32[256,1024]{1,0:T(8,128)}, bf16[256,1024]{1,0:T(8,128)(2,1)}) custom-call(bf16[16,16,1024]{2,1,0:T(8,128)(2,1)} %f_ref.1, f32[1,1024]{1,0:T(1,128)} %bitcast.4, f32[7,7,1024]{2,1,0:T(8,128)} %w_depth.1, bf16[1024,128]{1,0:T(8,128)(2,1)} %w_ref.1, f32[1,1024]{1,0:T(1,128)} %bitcast.5, f32[1,1024]{1,0:T(1,128)} %bitcast.6), custom_call_target="tpu_custom_call" | custom-call | tf_op jit(solution)/shard_map/layer/pallas_call | solution.py:472
  110.1 2.3 %add_convert_fusion = bf16[256,1024]{1,0:T(8,128)(2,1)} fusion(f32[256,1024]{1,0:T(8,128)} %get-tuple-element.7, bf16[256,1024]{1,0:T(8,128)(2,1)} %get-tuple-element.8), kind=kLoop, calls=%fused_computation | loop fusion | flops 786432 | bytes 2097152 | tf_op jit(solution)/shard_map/convert_element_type | solution.py:516
